TPU v7x, 128 devices: a whole 4x4x4 slice. The times are simulated.
128 devices in a mesh: expert: 32 (over z, x, core), replica: 4 (over y).
Axes of the slice: x: 4, y: 4, z: 4, core: 2. Of those that a mesh axis runs over, the one named last changes fastest.
Arguments:
- grad_out: bfloat16 [16384, 2048], P(('expert', 'replica')), may hold values from -6 to 6
- gates: bfloat16 [16384, 8], P(('expert', 'replica')), may hold values from 0.019897461 to 0.5
- experts: int32 [16384, 8], P(('expert', 'replica')), may hold values from 0 to 127, all different within a row; in each aligned block of 128 rows (0 to 127, 128 to 255, ...) at most 20 rows name the same one
- hidden: bfloat16 [128, 4, 640, 768], P('expert', 'replica'), may hold values from -6 to 6
- down_weight: bfloat16 [2048, 128, 768], P(None, 'expert'), may hold values from -0.21875 to 0.21875
Outputs:
- d_hidden: bfloat16 [128, 4, 640, 768], P('expert', 'replica')
- d_down: bfloat16 [2048, 128, 768], P('replica', 'expert')
- d_gates: float32 [16384, 8], P(('expert', 'replica'))
Inputs may be any that keep to these rules, and one draw needn't show every extreme that they name: Each token names 8 different experts. Among the 128 tokens of one device no expert is named by more than 20 tokens, a bound that some block reaches.
All inputs are finite; a program needn't handle non-finite values.
Results may differ from a plain program's by a relative error of at most 0.013.
Values may be sent and summed in bfloat16 or wider, within the bound.
A program may use at most 192 MiB of HBM per device.

v0:
```python
import jax
import jax.numpy as jnp
from jax import lax
from jax.sharding import PartitionSpec as P


def per_device(grad_out, gates, experts, hidden, down_weight):
    expert_count = lax.axis_size("expert")
    tok_rows = grad_out.shape[0]
    top_count = experts.shape[1]
    local_experts = hidden.shape[0]
    slot_count = hidden.shape[2]
    hidden_width = hidden.shape[3]
    capacity = slot_count // expert_count
    all_experts = local_experts * expert_count
    flat_ids = experts.reshape(-1)
    expert_range = jnp.arange(all_experts, dtype=jnp.int32)
    onehot_ids = (flat_ids[:, None] == expert_range[None, :]).astype(jnp.int32)
    running = jnp.cumsum(onehot_ids, axis=0)
    position = jnp.sum(onehot_ids * running, axis=1) - 1
    slot_index = (
        flat_ids % local_experts * expert_count + flat_ids // local_experts
    ) * capacity + position
    slot_index = slot_index.reshape(tok_rows, top_count)
    slot_range = jnp.arange(all_experts * capacity, dtype=jnp.int32)
    matches = slot_index[:, :, None] == slot_range[None, None, :]
    placing = jnp.any(matches, axis=1).astype(jnp.bfloat16)
    outgoing = jnp.einsum(
        "tr,td->rd", placing, grad_out, preferred_element_type=jnp.float32
    ).astype(jnp.bfloat16)
    out_gates = jnp.sum(
        jnp.where(matches, gates[:, :, None].astype(jnp.float32), 0.0), axis=(0, 1)
    ).astype(jnp.bfloat16)
    outgoing = outgoing.reshape(local_experts, expert_count, capacity, outgoing.shape[1])
    out_gates = out_gates.reshape(local_experts, expert_count, capacity)
    grad_slots, gate_slots = (
        lax.all_to_all(outgoing, "expert", split_axis=1, concat_axis=1, tiled=True),
        lax.all_to_all(out_gates, "expert", split_axis=1, concat_axis=1, tiled=True),
    )
    grad_slots = grad_slots.reshape(local_experts, slot_count, grad_slots.shape[3])
    gate_slots = gate_slots.reshape(local_experts, slot_count).astype(jnp.float32)
    hidden_slots = hidden.reshape(local_experts, slot_count, hidden_width)
    upstream = jnp.einsum(
        "esd,def->esf", grad_slots, down_weight, preferred_element_type=jnp.float32
    )
    hidden_grad = (gate_slots[:, :, None] * upstream).astype(jnp.bfloat16).reshape(hidden.shape)
    slot_grad = jnp.sum(hidden_slots.astype(jnp.float32) * upstream, axis=2)
    weighted = (gate_slots[:, :, None] * hidden_slots.astype(jnp.float32)).astype(jnp.bfloat16)
    down_grad = lax.psum_scatter(
        jnp.einsum("esd,esf->def", grad_slots, weighted, preferred_element_type=jnp.float32).astype(
            jnp.bfloat16
        ),
        "replica",
        scatter_dimension=0,
        tiled=True,
    )
    returned = lax.all_to_all(
        slot_grad.reshape(local_experts, expert_count, capacity),
        "expert",
        split_axis=1,
        concat_axis=1,
        tiled=True,
    )
    gate_grad = jnp.take(returned.reshape(-1), slot_index, axis=0)
    return (hidden_grad, down_grad, gate_grad)


def solution(mesh):
    in_specs = (
        P(("expert", "replica"), None),
        P(("expert", "replica"), None),
        P(("expert", "replica"), None),
        P("expert", "replica", None, None),
        P(None, "expert", None),
    )
    out_specs = (
        P("expert", "replica", None, None),
        P("replica", "expert", None),
        P(("expert", "replica"), None),
    )
    return jax.shard_map(
        per_device, mesh=mesh, in_specs=in_specs, out_specs=out_specs, check_vma=False
    )
```

profile of v0, /device:TPU:1, one launch (start us, length us, event | category | flops | bytes accessed | tf_op | source)
XLA Modules:
  0.0 347.1 jit_solution(9879499236836343738)
XLA Ops:
  7.2 0.0 copy-start
  7.2 0.8 copy.77
  8.0 0.1 eq.40
  8.1 0.1 eq.44
  8.2 0.1 copy.83
  8.3 0.8 copy.85
  9.1 0.2 fusion.15
  9.4 0.1 copy.84
  9.5 0.4 fusion.14
  9.9 0.1 sub.14
  10.0 0.1 compare_select_fusion
  10.1 1.6 select_reduce_fusion
  11.6 0.1 convert_element_type.52
  11.8 0.6 copy.86
  12.4 9.4 %all-to-all-start = ((bf16[4,32,20]{2,0,1:T(4,128)(2,1)}), bf16[4,32,20]{2,0,1:T(4,128)(2,1)S(1)}, u32[]{:S(2)}, u32[]{:S(2)}) async-start(bf16[4,32,20]{2,0,1:T(4,128)(2,1)} %copy.86), calls=%async_computation | async-start | bytes 65536 | tf_op jit(solution)/shard_map/all_to_all | solution.py:38
  21.8 5.0 %fusion.2 = pred[128,2560]{1,0:T(8,128)(4,1)S(1)} fusion(s32[128,8]{1,0:T(8,128)S(1)} %get-tuple-element.19), kind=kLoop, calls=%fused_computation.7 | loop fusion | flops 4915200 | bytes 331776 | tf_op jit(solution)/shard_map/reduce_or | solution.py:27
  26.8 0.0 copy-done
  26.8 5.5 %convolution_convert_fusion = bf16[2560,2048]{1,0:T(8,128)(2,1)} fusion(pred[128,2560]{1,0:T(8,128)(4,1)S(1)} %fusion.2, bf16[128,2048]{1,0:T(8,128)(2,1)S(1)} %copy-done), kind=kOutput, calls=%fused_computation.4 | convolution fusion | flops 1347420160 | bytes 11337728 | tf_op jit(solution)/shard_map/tr,td->rd/dot_general | solution.py:28
  32.4 16.4 %reshape.100 = bf16[4,32,20,2048]{3,2,1,0:T(8,128)(2,1)} reshape(bf16[2560,2048]{1,0:T(8,128)(2,1)} %convolution_convert_fusion) | data formatting | bytes 20971520 | tf_op jit(solution)/shard_map/reshape | solution.py:34
  48.7 13.7 %copy.89 = bf16[4,32,20,2048]{3,0,2,1:T(4,128)(2,1)} copy(bf16[4,32,20,2048]{3,2,1,0:T(8,128)(2,1)} %reshape.100) | data formatting | bytes 20971520 | tf_op jit(solution)/shard_map/reshape | solution.py:34
  62.4 0.0 all-to-all-done
  62.4 7.4 %all-to-all-start.1 = ((bf16[4,32,20,2048]{3,0,2,1:T(4,128)(2,1)}), bf16[4,32,20,2048]{3,0,2,1:T(4,128)(2,1)}, u32[]{:S(2)}, u32[]{:S(2)}) async-start(bf16[4,32,20,2048]{3,0,2,1:T(4,128)(2,1)} %copy.89), calls=%async_computation.1 | async-start | bytes 20971520 | tf_op jit(solution)/shard_map/all_to_all | solution.py:37
  69.9 0.2 reduce-scatter.2.cloned.1.call-start
  70.1 0.1 copy.87
  70.2 0.1 copy.88
  70.3 0.1 reshape.105
  70.4 125.4 %all-to-all-done.1 = bf16[4,32,20,2048]{3,0,2,1:T(4,128)(2,1)} async-done(((bf16[4,32,20,2048]{3,0,2,1:T(4,128)(2,1)}), bf16[4,32,20,2048]{3,0,2,1:T(4,128)(2,1)}, u32[]{:S(2)}, u32[]{:S(2)}) %all-to-all-start.1) | async-done | bytes 10485792 | tf_op jit(solution)/shard_map/all_to_all | solution.py:37
  195.8 20.0 %convert_bitcast_fusion = bf16[2048,4,768]{0,2,1:T(8,128)(2,1)} fusion(bf16[4,640,2048]{2,0,1:T(4,128)(2,1)} %bitcast.3, bf16[4,1,640,768]{3,2,1,0:T(8,128)(2,1)} %param.8, f32[4,640]{1,0:T(4,128)S(1)} %reshape.105), kind=kOutput, calls=%fused_computation.3 | convolution fusion | flops 8065253376 | bytes 27011072 | tf_op jit(solution)/shard_map/esd,esf->def/dot_general | solution.py:50
  215.8 0.0 reduce-scatter.2.cloned.1.call-update
  215.9 0.1 reshape.109
  216.0 35.2 %fusion.7 = (f32[4,640]{1,0:T(4,128)S(1)}, bf16[4,1,640,768]{3,2,1,0:T(8,128)(2,1)}) fusion(bf16[4,1,640,768]{3,2,1,0:T(8,128)(2,1)} %param.8, f32[4,640]{1,0:T(4,128)S(1)} %reshape.105, bf16[2048,4,768]{2,1,0:T(4,128)(2,1)} %param.9, bf16[4,640,2048]{2,0,1:T(4,128)(2,1)} %bitcast.3), kind=kOutput, calls=%fused_computation.14 | convolution fusion | flops 8062891520 | bytes 30953472 | tf_op jit(solution)/shard_map/esd,def->esf/dot_general | solution.py:43
  251.2 0.1 reshape.103
  251.3 0.7 copy.95
  252.0 10.6 %all-to-all-start.2 = ((f32[4,32,20]{2,0,1:T(4,128)}), f32[4,32,20]{2,0,1:T(4,128)S(1)}, u32[]{:S(2)}, u32[]{:S(2)}) async-start(f32[4,32,20]{2,0,1:T(4,128)} %copy.95), calls=%async_computation.3 | async-start | bytes 131072 | tf_op jit(solution)/shard_map/all_to_all | solution.py:57
  262.6 7.4 %all-to-all-done.2 = f32[4,32,20]{2,0,1:T(4,128)S(1)} async-done(((f32[4,32,20]{2,0,1:T(4,128)}), f32[4,32,20]{2,0,1:T(4,128)S(1)}, u32[]{:S(2)}, u32[]{:S(2)}) %all-to-all-start.2) | async-done | bytes 10272 | tf_op jit(solution)/shard_map/all_to_all | solution.py:57
  270.0 0.1 reshape.104
  270.1 0.0 copy-start.1
  270.1 6.2 %gather_fusion = f32[1024]{0:T(1024)S(1)} fusion(f32[2560]{0:T(1024)S(1)} %reshape.104, s32[1024]{0:T(1024)S(1)} %broadcast_clamp_fusion), kind=kCustom, calls=%fused_computation | custom fusion | bytes 12288 | tf_op jit(solution)/shard_map/jit(_take)/gather | solution.py:64
  276.3 0.1 reshape.108
  276.4 0.7 copy.99
  277.1 57.3 %reduce-scatter.2.cloned.1.call-done = bf16[512,4,768]{0,2,1:T(8,128)(2,1)} async-done(((bf16[2048,4,768]{0,2,1:T(8,128)(2,1)}), bf16[512,4,768]{0,2,1:T(8,128)(2,1)}) %reduce-scatter.2.cloned.1.call-update) | async-done | bytes 3145744 | tf_op jit(solution)/shard_map/reduce_scatter | solution.py:49
  334.3 6.0 %copy.98 = bf16[512,4,768]{2,1,0:T(4,128)(2,1)} copy(bf16[512,4,768]{0,2,1:T(8,128)(2,1)} %reduce-scatter.2.cloned.1.call-done) | data formatting | bytes 6291456
  340.3 0.0 copy-done.1
  (8 shorter events, 0.1 us)
Async XLA Ops:
  7.2 19.7 %copy-start = (bf16[128,2048]{1,0:T(8,128)(2,1)S(1)}, bf16[128,2048]{1,0:T(8,128)(2,1)}, u32[]{:S(2)}) copy-start(bf16[128,2048]{1,0:T(8,128)(2,1)} %param.5) | copy-start | bytes 1572868
  12.4 50.0 %all-to-all-start = ((bf16[4,32,20]{2,0,1:T(4,128)(2,1)}), bf16[4,32,20]{2,0,1:T(4,128)(2,1)S(1)}, u32[]{:S(2)}, u32[]{:S(2)}) async-start(bf16[4,32,20]{2,0,1:T(4,128)(2,1)} %copy.86), calls=%async_computation | async-start | bytes 65536 | tf_op jit(solution)/shard_map/all_to_all | solution.py:38
  62.4 133.4 %all-to-all-start.1 = ((bf16[4,32,20,2048]{3,0,2,1:T(4,128)(2,1)}), bf16[4,32,20,2048]{3,0,2,1:T(4,128)(2,1)}, u32[]{:S(2)}, u32[]{:S(2)}) async-start(bf16[4,32,20,2048]{3,0,2,1:T(4,128)(2,1)} %copy.89), calls=%async_computation.1 | async-start | bytes 20971520 | tf_op jit(solution)/shard_map/all_to_all | solution.py:37
  69.9 264.5 %reduce-scatter.2.cloned.1.call-start = ((), (), s32[]{:S(2)}) async-start(), calls=%async_computation.4 | async-start | bytes 15728640 | tf_op jit(solution)/shard_map/reduce_scatter | solution.py:49
  252.0 18.0 %all-to-all-start.2 = ((f32[4,32,20]{2,0,1:T(4,128)}), f32[4,32,20]{2,0,1:T(4,128)S(1)}, u32[]{:S(2)}, u32[]{:S(2)}) async-start(f32[4,32,20]{2,0,1:T(4,128)} %copy.95), calls=%async_computation.3 | async-start | bytes 131072 | tf_op jit(solution)/shard_map/all_to_all | solution.py:57
  270.1 70.2 %copy-start.1 = (bf16[128,2048]{1,0:T(8,128)(2,1)S(1)}, bf16[128,2048]{1,0:T(8,128)(2,1)}, u32[]{:S(2)}) copy-start(bf16[128,2048]{1,0:T(8,128)(2,1)} %param.5) | copy-start | bytes 1572868
Sparse Core Ops, SparseCore 0:
  216.0 118.2 reduce-scatter.1
where the time goes:
time: 348 us; the launch traced here: 347 us
  waiting for transfers between devices  190 us (55%)
  matrix products  60.8 us (17%)
  local copies, waits for them, and re-layouts  47.1 us (14%)
  starting transfers between devices  27.7 us (8%)
  between operations  14.2 us (4%)
  other arithmetic  7.29 us (2%)
    all_to_all x1, waiting for transfers between devices, per_device(): lax.all_to_all(outgoing, 'expert', split_axis=1, concat_axis=1, tiled=True)  125 us
    reduce_scatter x1, waiting for transfers between devices, per_device(): lax.psum_scatter(jnp.einsum('esd,esf->def', grad_slots, weighted, preferr...  57.3 us
    dot_general x1, matrix products, per_device(): jnp.einsum('esd,def->esf', grad_slots, down_weight, preferred_element_typ...  35.2 us
    reshape x2, local copies, waits for them, and re-layouts, per_device(): outgoing.reshape(local_experts, expert_count, capacity, outgoing.shape[1])  30.1 us
    dot_general x1, matrix products, per_device(): jnp.einsum('esd,esf->def', grad_slots, weighted, preferred_element_type=j...  20 us
    all_to_all x1, starting transfers between devices, per_device(): lax.all_to_all(slot_grad.reshape(local_experts, expert_count, capacity),...  10.6 us
    all_to_all x1, starting transfers between devices, per_device(): lax.all_to_all(out_gates, 'expert', split_axis=1, concat_axis=1, tiled=True)  9.43 us
    unnamed x7, local copies, waits for them, and re-layouts  7.48 us
  transfers between devices with their start and end apart: 4, of which 3 were waited for; matrix products, arithmetic and copies ran while one was open for 24% of the time, Pallas kernels for 0%

commit v1 on v0

--- a/solution.py
+++ b/solution.py
@@ -34,7 +34,12 @@
     outgoing = outgoing.reshape(local_experts, expert_count, capacity, outgoing.shape[1])
     out_gates = out_gates.reshape(local_experts, expert_count, capacity)
     grad_slots, gate_slots = (
-        lax.all_to_all(outgoing, "expert", split_axis=1, concat_axis=1, tiled=True),
+        jnp.concatenate(
+            lax.all_to_all(
+                jnp.stack(jnp.split(outgoing, lax.axis_size("expert"), axis=1)), "expert", 0, 0
+            ),
+            axis=1,
+        ),
         lax.all_to_all(out_gates, "expert", split_axis=1, concat_axis=1, tiled=True),
     )
     grad_slots = grad_slots.reshape(local_experts, slot_count, grad_slots.shape[3])

time: 348 us -> 392 us (1.13)
  local copies, waits for them, and re-layouts: 47.1 us -> 89.9 us
    unnamed x7 -> x38, local copies, waits for them, and re-layouts: 7.48 us -> 39.3 us
    another operation x3 -> x5, local copies, waits for them, and re-layouts: 0.11 us -> 24.8 us  [the longest x2 24.7 us: per_device(): jnp.stack(jnp.split(outgoing, lax.axis_size('expert'), axis=1))]
    reshape x2 -> x1, local copies, waits for them, and re-layouts: 30.1 us -> 16.4 us  [per_device(): outgoing.reshape(local_experts, expert_count, capacity, outgoing.shape[1])]
  transfers between devices with their start and end apart: 4 -> 4, of which waited for: 3 -> 3; matrix products, arithmetic and copies ran while one was open for 24% -> 33% of each run, Pallas kernels for 0% -> 0%
where the time goes in v1:
time: 392 us; the launch traced here: 390 us
  waiting for transfers between devices  190 us (48%)
  local copies, waits for them, and re-layouts  89.9 us (23%)
  matrix products  60.8 us (16%)
  starting transfers between devices  27.7 us (7%)
  between operations  14.3 us (4%)
  other arithmetic  7.29 us (2%)
    all_to_all x1, waiting for transfers between devices, per_device(): lax.all_to_all(jnp.stack(jnp.split(outgoing, lax.axis_size('expert'), axi...  125 us
    reduce_scatter x1, waiting for transfers between devices, per_device(): lax.psum_scatter(jnp.einsum('esd,esf->def', grad_slots, weighted, preferr...  57.2 us
    unnamed x38, local copies, waits for them, and re-layouts  39.3 us
    dot_general x1, matrix products, per_device(): jnp.einsum('esd,def->esf', grad_slots, down_weight, preferred_element_typ...  35.3 us
    another operation x2, local copies, waits for them, and re-layouts, per_device(): jnp.stack(jnp.split(outgoing, lax.axis_size('expert'), axis=1))  24.7 us
    dot_general x1, matrix products, per_device(): jnp.einsum('esd,esf->def', grad_slots, weighted, preferred_element_type=j...  20 us
    reshape x1, local copies, waits for them, and re-layouts, per_device(): outgoing.reshape(local_experts, expert_count, capacity, outgoing.shape[1])  16.4 us
    all_to_all x1, starting transfers between devices, per_device(): lax.all_to_all(slot_grad.reshape(local_experts, expert_count, capacity),...  10.6 us
  transfers between devices with their start and end apart: 4, of which 3 were waited for; matrix products, arithmetic and copies ran while one was open for 33% of the time, Pallas kernels for 0%

profile of v1, /device:TPU:1, one launch (start us, length us, event | category | flops | bytes accessed | tf_op | source)
XLA Modules:
  0.0 390.1 jit_solution(14297181798882759407)
XLA Ops:
  7.2 0.8 copy.202
  8.0 0.1 eq.40
  8.2 0.1 copy.208
  8.3 0.8 copy.210
  9.1 0.2 fusion.15
  9.4 0.1 copy.209
  9.5 0.4 fusion.14
  10.1 1.6 select_reduce_fusion
  11.6 0.1 convert_element_type.52
  11.8 0.6 copy.211
  12.4 9.4 %all-to-all-start = ((bf16[4,32,20]{2,0,1:T(4,128)(2,1)}), bf16[4,32,20]{2,0,1:T(4,128)(2,1)S(1)}, u32[]{:S(2)}, u32[]{:S(2)}) async-start(bf16[4,32,20]{2,0,1:T(4,128)(2,1)} %copy.211), calls=%async_computation | async-start | bytes 65536 | tf_op jit(solution)/shard_map/all_to_all | solution.py:43
  21.8 5.0 %fusion.2 = pred[128,2560]{1,0:T(8,128)(4,1)S(1)} fusion(s32[128,8]{1,0:T(8,128)S(1)} %get-tuple-element.19), kind=kLoop, calls=%fused_computation.7 | loop fusion | flops 4915200 | bytes 331776 | tf_op jit(solution)/shard_map/reduce_or | solution.py:27
  26.8 5.5 %convolution_convert_fusion = bf16[2560,2048]{1,0:T(8,128)(2,1)} fusion(pred[128,2560]{1,0:T(8,128)(4,1)S(1)} %fusion.2, bf16[128,2048]{1,0:T(8,128)(2,1)S(1)} %copy-done), kind=kOutput, calls=%fused_computation.4 | convolution fusion | flops 1347420160 | bytes 11337728 | tf_op jit(solution)/shard_map/tr,td->rd/dot_general | solution.py:28
  32.4 16.4 %reshape.100 = bf16[4,32,20,2048]{3,2,1,0:T(8,128)(2,1)} reshape(bf16[2560,2048]{1,0:T(8,128)(2,1)} %convolution_convert_fusion) | data formatting | bytes 20971520 | tf_op jit(solution)/shard_map/reshape | solution.py:34
  48.7 1.0 fusion.48
  49.8 1.0 fusion.47
  50.8 1.0 fusion.46
  51.8 1.0 fusion.45
  52.8 1.0 fusion.44
  53.9 1.0 fusion.43
  54.9 1.0 fusion.42
  55.9 1.0 fusion.41
  57.0 1.0 fusion.40
  58.0 1.0 fusion.39
  59.0 1.0 fusion.38
  60.1 1.0 fusion.37
  61.1 1.0 fusion.36
  62.1 1.0 fusion.35
  63.2 1.0 fusion.34
  64.2 1.0 fusion.33
  65.2 1.0 fusion.32
  66.3 1.0 fusion.31
  67.3 1.0 fusion.30
  68.3 1.0 fusion.29
  69.4 1.0 fusion.28
  70.4 1.0 fusion.27
  71.4 1.0 fusion.26
  72.4 1.0 fusion.25
  73.5 1.0 fusion.24
  74.5 1.0 fusion.23
  75.5 1.0 fusion.22
  76.6 1.0 fusion.21
  77.6 1.0 fusion.20
  78.6 1.0 fusion.19
  79.7 1.0 fusion.18
  80.7 1.0 fusion.17
  81.7 23.6 %copy.245 = bf16[32,4,1,20,2048]{4,1,3,2,0:T(4,128)(2,1)} copy(bf16[32,4,1,20,2048]{4,3,1,2,0:T(8,128)(2,1)S(1)} %fusion.17) | data formatting | bytes 20971520 | tf_op jit(solution)/shard_map/stack | solution.py:39
  105.4 7.4 %all-to-all-start.1 = ((bf16[32,4,1,20,2048]{4,1,3,2,0:T(4,128)(2,1)}), bf16[32,4,1,20,2048]{4,1,3,2,0:T(4,128)(2,1)}, u32[]{:S(2)}, u32[]{:S(2)}) async-start(bf16[32,4,1,20,2048]{4,1,3,2,0:T(4,128)(2,1)} %copy.245), calls=%async_computation.1 | async-start | bytes 20971520 | tf_op jit(solution)/shard_map/all_to_all | solution.py:38
  112.8 0.3 reduce-scatter.2.cloned.1.call-start
  113.1 0.1 copy.212
  113.2 0.1 copy.213
  113.3 0.1 reshape.105
  113.4 125.4 %all-to-all-done.1 = bf16[32,4,1,20,2048]{4,1,3,2,0:T(4,128)(2,1)} async-done(((bf16[32,4,1,20,2048]{4,1,3,2,0:T(4,128)(2,1)}), bf16[32,4,1,20,2048]{4,1,3,2,0:T(4,128)(2,1)}, u32[]{:S(2)}, u32[]{:S(2)}) %all-to-all-start.1) | async-done | bytes 10485792 | tf_op jit(solution)/shard_map/all_to_all | solution.py:38
  238.8 20.0 %convert_bitcast_fusion = bf16[2048,4,768]{0,2,1:T(8,128)(2,1)} fusion(bf16[4,640,2048]{2,0,1:T(4,128)(2,1)} %bitcast.36, bf16[4,1,640,768]{3,2,1,0:T(8,128)(2,1)} %param.8, f32[4,640]{1,0:T(4,128)S(1)} %reshape.105), kind=kOutput, calls=%fused_computation.3 | convolution fusion | flops 8065253376 | bytes 27011072 | tf_op jit(solution)/shard_map/esd,esf->def/dot_general | solution.py:55
  258.9 35.3 %fusion.7 = (f32[4,640]{1,0:T(4,128)S(1)}, bf16[4,1,640,768]{3,2,1,0:T(8,128)(2,1)}) fusion(bf16[4,1,640,768]{3,2,1,0:T(8,128)(2,1)} %param.8, f32[4,640]{1,0:T(4,128)S(1)} %reshape.105, bf16[2048,4,768]{2,1,0:T(4,128)(2,1)} %param.9, bf16[4,640,2048]{2,0,1:T(4,128)(2,1)} %bitcast.36), kind=kOutput, calls=%fused_computation.14 | convolution fusion | flops 8062891520 | bytes 30953472 | tf_op jit(solution)/shard_map/esd,def->esf/dot_general | solution.py:48
  294.2 0.1 reshape.103
  294.3 0.7 copy.251
  295.0 10.6 %all-to-all-start.2 = ((f32[4,32,20]{2,0,1:T(4,128)}), f32[4,32,20]{2,0,1:T(4,128)S(1)}, u32[]{:S(2)}, u32[]{:S(2)}) async-start(f32[4,32,20]{2,0,1:T(4,128)} %copy.251), calls=%async_computation.3 | async-start | bytes 131072 | tf_op jit(solution)/shard_map/all_to_all | solution.py:62
  305.6 7.4 %all-to-all-done.2 = f32[4,32,20]{2,0,1:T(4,128)S(1)} async-done(((f32[4,32,20]{2,0,1:T(4,128)}), f32[4,32,20]{2,0,1:T(4,128)S(1)}, u32[]{:S(2)}, u32[]{:S(2)}) %all-to-all-start.2) | async-done | bytes 10272 | tf_op jit(solution)/shard_map/all_to_all | solution.py:62
  313.0 0.1 reshape.104
  313.2 6.2 %gather_fusion = f32[1024]{0:T(1024)S(1)} fusion(f32[2560]{0:T(1024)S(1)} %reshape.104, s32[1024]{0:T(1024)S(1)} %broadcast_clamp_fusion), kind=kCustom, calls=%fused_computation | custom fusion | bytes 12288 | tf_op jit(solution)/shard_map/jit(_take)/gather | solution.py:69
  319.4 0.7 copy.255
  320.1 57.2 %reduce-scatter.2.cloned.1.call-done = bf16[512,4,768]{0,2,1:T(8,128)(2,1)} async-done(((bf16[2048,4,768]{0,2,1:T(8,128)(2,1)}), bf16[512,4,768]{0,2,1:T(8,128)(2,1)}) %reduce-scatter.2.cloned.1.call-update) | async-done | bytes 3145744 | tf_op jit(solution)/shard_map/reduce_scatter | solution.py:54
  377.3 6.0 %copy.254 = bf16[512,4,768]{2,1,0:T(4,128)(2,1)} copy(bf16[512,4,768]{0,2,1:T(8,128)(2,1)} %reduce-scatter.2.cloned.1.call-done) | data formatting | bytes 6291456
  (19 shorter events, 0.6 us)
Async XLA Ops:
  7.2 19.7 %copy-start = (bf16[128,2048]{1,0:T(8,128)(2,1)S(1)}, bf16[128,2048]{1,0:T(8,128)(2,1)}, u32[]{:S(2)}) copy-start(bf16[128,2048]{1,0:T(8,128)(2,1)} %param.5) | copy-start | bytes 1572868
  12.4 93.0 %all-to-all-start = ((bf16[4,32,20]{2,0,1:T(4,128)(2,1)}), bf16[4,32,20]{2,0,1:T(4,128)(2,1)S(1)}, u32[]{:S(2)}, u32[]{:S(2)}) async-start(bf16[4,32,20]{2,0,1:T(4,128)(2,1)} %copy.211), calls=%async_computation | async-start | bytes 65536 | tf_op jit(solution)/shard_map/all_to_all | solution.py:43
  105.4 133.4 %all-to-all-start.1 = ((bf16[32,4,1,20,2048]{4,1,3,2,0:T(4,128)(2,1)}), bf16[32,4,1,20,2048]{4,1,3,2,0:T(4,128)(2,1)}, u32[]{:S(2)}, u32[]{:S(2)}) async-start(bf16[32,4,1,20,2048]{4,1,3,2,0:T(4,128)(2,1)} %copy.245), calls=%async_computation.1 | async-start | bytes 20971520 | tf_op jit(solution)/shard_map/all_to_all | solution.py:38
  112.8 264.5 %reduce-scatter.2.cloned.1.call-start = ((), (), s32[]{:S(2)}) async-start(), calls=%async_computation.4 | async-start | bytes 15728640 | tf_op jit(solution)/shard_map/reduce_scatter | solution.py:54
  295.0 18.0 %all-to-all-start.2 = ((f32[4,32,20]{2,0,1:T(4,128)}), f32[4,32,20]{2,0,1:T(4,128)S(1)}, u32[]{:S(2)}, u32[]{:S(2)}) async-start(f32[4,32,20]{2,0,1:T(4,128)} %copy.251), calls=%async_computation.3 | async-start | bytes 131072 | tf_op jit(solution)/shard_map/all_to_all | solution.py:62
  313.1 70.1 %copy-start.1 = (bf16[128,2048]{1,0:T(8,128)(2,1)S(1)}, bf16[128,2048]{1,0:T(8,128)(2,1)}, u32[]{:S(2)}) copy-start(bf16[128,2048]{1,0:T(8,128)(2,1)} %param.5) | copy-start | bytes 1572868
Sparse Core Ops, SparseCore 0:
  259.0 118.2 reduce-scatter.1
